TPU v7x, 32 devices: a whole 2x2x4 slice. The times are simulated.
32 devices in a mesh: blk: 8 (over z, x), sub: 4 (over y, core).
Axes of the slice: x: 2, y: 2, z: 4, core: 2. Of those that a mesh axis runs over, the one named last changes fastest.
Arguments:
- features: bfloat16 [12288, 768], P(('blk', 'sub')), may hold values from -6 to 6
- scales: bfloat16 [12288], P('blk'), may hold values from 0.5 to 4
- neighbor_lists: int32 [9, 16, 12288], P(None, None, 'blk'), may hold values from 0 to 1535, as said below
- eigen_block: float32 [64, 12288], P(None, ('blk', 'sub')), may hold values from -6 to 6
Outputs:
- embedding: float32 [64, 12288], P(None, ('blk', 'sub'))
Inputs may be any that keep to these rules, and one draw needn't show every extreme that they name: For each j and point p, the 16 entries neighbor_lists[j, :, p] are distinct positions within the row block that lies j - 4 blocks before p's block, counted cyclically.
All inputs are finite; a program needn't handle non-finite values.
Results may differ from a plain program's by a relative error of at most 0.0039.
Values may be sent and summed in bfloat16 or wider, within the bound.
A program may use at most 128 MiB of HBM per device.

v0:
```python
import math

import jax
import jax.numpy as jnp
from jax import lax
from jax.sharding import PartitionSpec as P

F = 768


def as_sent(value):
    return jax.tree.map(lambda a: a.astype(jnp.bfloat16) if a.dtype == jnp.float32 else a, value)


def shifted(value, axis, steps):
    count = lax.axis_size(axis)
    pairs = [(source, (source + steps) % count) for source in range(count)]
    return lax.ppermute(value, axis, pairs)


def pair_weights(
    block_feats, block_norms, block_scales, lists_here, positions, moving_feats, moving_scales
):
    inner = lax.dot_general(
        block_feats, moving_feats, (((1,), (1,)), ((), ())), preferred_element_type=jnp.float32
    )
    moving_norms = jnp.sum(jnp.square(moving_feats.astype(jnp.float32)), axis=1)
    distance = block_norms[:, None] + moving_norms[None, :] - 2.0 * inner
    spread = F * block_scales[:, None] * moving_scales.astype(jnp.float32)[None, :]
    affinity = jnp.exp(-distance / spread)
    listed = jnp.sum(
        (lists_here[:, :, None] == positions[None, None, :]).astype(jnp.float32), axis=0
    )
    return affinity * listed


def band_sweep(payload, work, half):
    row_total, col_total = work(half, payload)
    for heading in (1, -1):
        pieces = payload
        owed = []
        for travel in range(1, half + 1):
            pieces = jax.tree.map(
                lambda part, own: part.astype(own.dtype),
                shifted(as_sent(pieces), "blk", heading),
                pieces,
            )
            row_term, col_term = work(heading * travel + half, pieces)
            row_total = row_total + row_term
            owed.append(col_term)
        carried = jnp.zeros_like(owed[0])
        for travel in range(half - 1, -1, -1):
            carried = shifted(carried + owed[travel], "blk", -heading)
        col_total = col_total + carried
    return (row_total, col_total)


def to_owners(terms):
    return lax.psum_scatter(terms, "sub", scatter_dimension=1, tiled=True)


def local(features, scales, neighbor_lists, eigen_block):
    rows_dev = features.shape[0]
    sub_index = lax.axis_index("sub")
    half = (neighbor_lists.shape[0] - 1) // 2
    block_feats = lax.all_gather(features, "sub", axis=0, tiled=True)
    block_norms = jnp.sum(jnp.square(block_feats.astype(jnp.float32)), axis=1)
    block_scales = scales.astype(jnp.float32)
    own_scales = lax.dynamic_slice_in_dim(scales, sub_index * rows_dev, rows_dev)
    positions = sub_index * rows_dev + jnp.arange(rows_dev, dtype=jnp.int32)

    def weights(shift_index, pieces):
        return pair_weights(
            block_feats,
            block_norms,
            block_scales,
            neighbor_lists[shift_index],
            positions,
            pieces[0],
            pieces[1],
        )

    def degree_work(shift_index, pieces):
        tile = weights(shift_index, pieces)
        return (jnp.sum(tile, axis=1)[None, :], jnp.sum(tile, axis=0)[None, :])

    row_deg, col_deg = band_sweep((features, own_scales), degree_work, half)
    degree = 1.0 + 0.5 * (to_owners(row_deg) + col_deg)
    inv_root = lax.rsqrt(degree)
    scaled = eigen_block * inv_root
    scaled_low = scaled.astype(jnp.bfloat16)
    block_eigen = lax.all_gather(scaled_low, "sub", axis=1, tiled=True)

    def product_work(shift_index, pieces):
        tile = weights(shift_index, pieces).astype(jnp.bfloat16)
        moving_eigen = pieces[2]
        row_term = lax.dot_general(
            moving_eigen, tile, (((1,), (1,)), ((), ())), preferred_element_type=jnp.float32
        )
        col_term = jnp.dot(block_eigen, tile, preferred_element_type=jnp.float32)
        return (row_term, col_term)

    product_payload = (features, own_scales, scaled_low)
    row_side, col_side = band_sweep(product_payload, product_work, half)
    mixed = inv_root * (scaled + 0.5 * (to_owners(row_side) + col_side))
    partial_gram = jnp.dot(
        mixed, mixed.T, precision=lax.Precision.HIGHEST, preferred_element_type=jnp.float32
    )
    gram = lax.psum(partial_gram, ("blk", "sub"))
    lower = jnp.linalg.cholesky(gram)
    total_rows = rows_dev * lax.axis_size("blk") * lax.axis_size("sub")
    return math.sqrt(total_rows) * jax.scipy.linalg.solve_triangular(lower, mixed, lower=True)


def solution(mesh):
    placed = (P(("blk", "sub"), None), P("blk"), P(None, None, "blk"), P(None, ("blk", "sub")))
    return jax.shard_map(
        local, mesh=mesh, in_specs=placed, out_specs=P(None, ("blk", "sub")), check_vma=False
    )
```

profile of v0, /device:TPU:0, one launch (start us, length us, event | category | flops | bytes accessed | tf_op | source)
XLA Modules:
  0.0 343.8 jit_solution(11951891037983374221)
XLA Ops:
  18.1 17.8 %collective-permute-done.1 = bf16[384]{0:T(512)(128)(2,1)S(1)} collective-permute-done((bf16[384]{0:T(512)(128)(2,1)S(1)}, bf16[384]{0:T(512)(128)(2,1)S(1)}, u32[]{:S(2)}, u32[]{:S(2)}) %collective-permute-start.1) | collective-permute-done | bytes 800 | tf_op jit(solution)/shard_map/ppermute | solution.py:18
  41.4 4.7 %collective-permute-start.10 = (bf16[384,768]{1,0:T(8,128)(2,1)S(1)}, bf16[384,768]{1,0:T(8,128)(2,1)S(1)}, u32[]{:S(2)}, u32[]{:S(2)}) collective-permute-start(bf16[384,768]{1,0:T(8,128)(2,1)S(1)} %collective-permute-done.8), channel_id=1, source_target_pairs={{0,28},{4,0},{8,4},{12,8},{16,12},{20,16},{24,20},{28,24},{1,29},{... | collective-permute-start | bytes 1769480 | tf_op jit(solution)/shard_map/ppermute | solution.py:18
  46.1 44.8 %convert_reduce_fusion.7 = (f32[1536,384]{1,0:T(8,128)}, f32[1536,384]{1,0:T(8,128)}, f32[1536,384]{1,0:T(8,128)}, f32[1536,384]{1,0:T(8,128)}, f32[1536,384]{1,...) fusion(s32[16,1536]{1,0:T(8,128)S(1)} %get-tuple-element.40, ...), kind=kLoop, calls=%fused_computation.7 | loop fusion | flops 249495552 | bytes 22119936 | tf_op jit(solution)/shard_map/reduce_sum | solution.py:31
  90.9 4.7 %collective-permute-start.13 = (bf16[384]{0:T(512)(128)(2,1)S(1)}, bf16[384]{0:T(512)(128)(2,1)S(1)}, u32[]{:S(2)}, u32[]{:S(2)}) collective-permute-start(bf16[384]{0:T(512)(128)(2,1)S(1)} %collective-permute-done.11), channel_id=1, source_target_pairs={{0,28},{4,0},{8,4},{12,8},{16,12},{20,16},{24,20},{28,24},{1,29},{... | collective-permute-start | bytes 2312 | tf_op jit(solution)/shard_map/ppermute | solution.py:18
  97.2 4.7 %collective-permute-start.15 = (bf16[384]{0:T(512)(128)(2,1)S(1)}, bf16[384]{0:T(512)(128)(2,1)S(1)}, u32[]{:S(2)}, u32[]{:S(2)}) collective-permute-start(bf16[384]{0:T(512)(128)(2,1)S(1)} %collective-permute-done.13), channel_id=1, source_target_pairs={{0,28},{4,0},{8,4},{12,8},{16,12},{20,16},{24,20},{28,24},{1,29},{... | collective-permute-start | bytes 2312 | tf_op jit(solution)/shard_map/ppermute | solution.py:18
  106.1 12.8 %collective-permute-done.7 = bf16[384]{0:T(512)(128)(2,1)S(1)} collective-permute-done((bf16[384]{0:T(512)(128)(2,1)S(1)}, bf16[384]{0:T(512)(128)(2,1)S(1)}, u32[]{:S(2)}, u32[]{:S(2)}) %collective-permute-start.7) | collective-permute-done | bytes 800 | tf_op jit(solution)/shard_map/ppermute | solution.py:18
  124.5 12.0 %collective-permute-done.12 = bf16[384,768]{1,0:T(8,128)(2,1)S(1)} collective-permute-done((bf16[384,768]{1,0:T(8,128)(2,1)S(1)}, bf16[384,768]{1,0:T(8,128)(2,1)S(1)}, u32[]{:S(2)}, u32[]{:S(2)}) %collective-permute-start.12) | collective-permute-done | bytes 589856 | tf_op jit(solution)/shard_map/ppermute | solution.py:18
  138.8 7.2 %collective-permute-done.6 = bf16[384,768]{1,0:T(8,128)(2,1)S(1)} collective-permute-done((bf16[384,768]{1,0:T(8,128)(2,1)S(1)}, bf16[384,768]{1,0:T(8,128)(2,1)S(1)}, u32[]{:S(2)}, u32[]{:S(2)}) %collective-permute-start.6) | collective-permute-done | bytes 589856 | tf_op jit(solution)/shard_map/ppermute | solution.py:18
  146.8 4.9 %collective-permute-done.14 = bf16[384,768]{1,0:T(8,128)(2,1)S(1)} collective-permute-done((bf16[384,768]{1,0:T(8,128)(2,1)S(1)}, bf16[384,768]{1,0:T(8,128)(2,1)S(1)}, u32[]{:S(2)}, u32[]{:S(2)}) %collective-permute-start.14) | collective-permute-done | bytes 589856 | tf_op jit(solution)/shard_map/ppermute | solution.py:18
  155.7 4.2 %fusion.40 = (f32[384]{0:T(512)S(1)}, f32[1536]{0:T(1024)S(1)}, bf16[1536,384]{1,0:T(8,128)(2,1)S(1)}) fusion(f32[1536,384]{1,0:T(8,128)} %get-tuple-element.26, f32[384]{0:T(512)} %convert_element_type.159, f32[1536]{0:T(1024)S(1)} %convert_multiply_fusion, bf16[1536,768]{1,0:T(8,128)(2,1)S(1)} %copy-done.8, bf16[384,768]{1,0:T(8,128)(2,1)} %copy-done.26, ...), kind=kOutput, calls=%fused_computation.114 | convolution fusion | flops 911865984 | bytes 6511104 | tf_op jit(solution)/shard_map/dot_general | solution.py:24
  183.6 4.1 %fusion.42 = (f32[384]{0:T(512)}, f32[1536]{0:T(1024)S(1)}, bf16[1536,384]{1,0:T(8,128)(2,1)}) fusion(f32[1536,384]{1,0:T(8,128)S(1)} %copy-done.12, f32[384]{0:T(512)S(1)} %copy-done.37, f32[1536]{0:T(1024)S(1)} %convert_multiply_fusion, bf16[1536,768]{1,0:T(8,128)(2,1)S(1)} %copy-done.8, bf16[384,768]{1,0:T(8,128)(2,1)S(1)} %collective-permute-done.10, ...), kind=kOutput, calls=%fused_computation.116 | convolution fusion | flops 911865984 | bytes 6511104 | tf_op jit(solution)/shard_map/dot_general | solution.py:24
  195.7 4.7 %collective-permute-start.17 = (f32[1,384]{1,0:T(1,128)S(1)}, f32[1,384]{1,0:T(1,128)S(1)}, u32[]{:S(2)}, u32[]{:S(2)}) collective-permute-start(f32[1,384]{1,0:T(1,128)S(1)} %reshape_add_fusion.5), channel_id=1, source_target_pairs={{0,28},{4,0},{8,4},{12,8},{16,12},{20,16},{24,20},{28,24},{1,29},{... | collective-permute-start | bytes 4616 | tf_op jit(solution)/shard_map/ppermute | solution.py:18
  201.7 5.0 %collective-permute-start.18 = (f32[1,384]{1,0:T(1,128)S(1)}, f32[1,384]{1,0:T(1,128)S(1)}, u32[]{:S(2)}, u32[]{:S(2)}) collective-permute-start(f32[1,384]{1,0:T(1,128)S(1)} %reshape_add_fusion.4), channel_id=1, source_target_pairs={{0,28},{4,0},{8,4},{12,8},{16,12},{20,16},{24,20},{28,24},{1,29},{... | collective-permute-start | bytes 4616 | tf_op jit(solution)/shard_map/ppermute | solution.py:18
  208.0 5.0 %collective-permute-start.19 = (f32[1,384]{1,0:T(1,128)S(1)}, f32[1,384]{1,0:T(1,128)S(1)}, u32[]{:S(2)}, u32[]{:S(2)}) collective-permute-start(f32[1,384]{1,0:T(1,128)S(1)} %reshape_add_fusion.3), channel_id=1, source_target_pairs={{0,28},{4,0},{8,4},{12,8},{16,12},{20,16},{24,20},{28,24},{1,29},{... | collective-permute-start | bytes 4616 | tf_op jit(solution)/shard_map/ppermute | solution.py:18
  213.7 6.1 %reduce-scatter.7.cloned.1.call-done = f32[384,1]{1,0:T(8,128)} async-done(((f32[1536,1]{1,0:T(8,128)}), f32[384,1]{1,0:T(8,128)}) %reduce-scatter.7.cloned.1.call-update) | async-done | bytes 1552
  220.9 5.7 %all_gather.7 = bf16[64,1536]{1,0:T(8,128)(2,1)S(1)} all-gather(bf16[64,384]{1,0:T(8,128)(2,1)S(1)} %multiply_convert_fusion), channel_id=1, replica_groups=mesh['blk'=8,'sub'=4] {'sub'}, dimensions={1}, use_global_device_ids=true | all-gather | bytes 245760 | tf_op jit(solution)/shard_map/all_gather | solution.py:92
  238.4 4.8 %collective-permute-start.29 = (bf16[64,384]{1,0:T(8,128)(2,1)S(1)}, bf16[64,384]{1,0:T(8,128)(2,1)S(1)}, u32[]{:S(2)}, u32[]{:S(2)}) collective-permute-start(bf16[64,384]{1,0:T(8,128)(2,1)S(1)} %collective-permute-done.28), channel_id=1, source_target_pairs={{0,28},{4,0},{8,4},{12,8},{16,12},{20,16},{24,20},{28,24},{1,29},{... | collective-permute-start | bytes 147464 | tf_op jit(solution)/shard_map/ppermute | solution.py:18
  245.4 4.8 %collective-permute-start.30 = (bf16[64,384]{1,0:T(8,128)(2,1)S(1)}, bf16[64,384]{1,0:T(8,128)(2,1)S(1)}, u32[]{:S(2)}, u32[]{:S(2)}) collective-permute-start(bf16[64,384]{1,0:T(8,128)(2,1)S(1)} %collective-permute-done.29), channel_id=1, source_target_pairs={{0,28},{4,0},{8,4},{12,8},{16,12},{20,16},{24,20},{28,24},{1,29},{... | collective-permute-start | bytes 147464 | tf_op jit(solution)/shard_map/ppermute | solution.py:18
  264.7 4.8 %collective-permute-start.34 = (f32[64,384]{1,0:T(8,128)S(1)}, f32[64,384]{1,0:T(8,128)S(1)}, u32[]{:S(2)}, u32[]{:S(2)}) collective-permute-start(f32[64,384]{1,0:T(8,128)S(1)} %add.427), channel_id=1, source_target_pairs={{0,28},{4,0},{8,4},{12,8},{16,12},{20,16},{24,20},{28,24},{1,29},{... | collective-permute-start | bytes 294920 | tf_op jit(solution)/shard_map/ppermute | solution.py:18
  271.7 5.2 %collective-permute-start.35 = (f32[64,384]{1,0:T(8,128)S(1)}, f32[64,384]{1,0:T(8,128)S(1)}, u32[]{:S(2)}, u32[]{:S(2)}) collective-permute-start(f32[64,384]{1,0:T(8,128)S(1)} %add.428), channel_id=1, source_target_pairs={{0,28},{4,0},{8,4},{12,8},{16,12},{20,16},{24,20},{28,24},{1,29},{... | collective-permute-start | bytes 294920 | tf_op jit(solution)/shard_map/ppermute | solution.py:18
  279.1 6.8 %collective-permute-done.39 = f32[64,384]{1,0:T(8,128)S(1)} collective-permute-done((f32[64,384]{1,0:T(8,128)S(1)}, f32[64,384]{1,0:T(8,128)S(1)}, u32[]{:S(2)}, u32[]{:S(2)}) %collective-permute-start.39) | collective-permute-done | bytes 98336 | tf_op jit(solution)/shard_map/ppermute | solution.py:18
  287.2 37.0 %psum.7 = f32[64,64]{0,1:T(8,128)S(1)} all-reduce(f32[64,64]{0,1:T(8,128)S(1)} %fusion.46), channel_id=1, replica_groups=mesh['blk'=8,'sub'=4] {'blk','sub'}, use_global_device_ids=true, to_apply=%region_39.0 | all-reduce | flops 4096 | bytes 32768 | tf_op jit(solution)/shard_map/psum | solution.py:109
  324.2 5.8 %cholesky.16 = f32[64,64]{1,0:T(8,128)S(1)} custom-call(f32[64,64]{1,0:T(8,128)S(1)} %fusion.35), custom_call_target="Cholesky" | custom-call | tf_op jit(solution)/shard_map/jit(cholesky)/cholesky | solution.py:110
  331.4 4.9 %custom-call.7 = f32[1,64,64]{1,2,0:T(8,128)S(1)} custom-call(f32[1,64,64]{2,1,0:T(8,128)S(1)} %fusion.33), custom_call_target="InvertDiagBlocksLowerTriangular" | custom-call | tf_op jit(solution)/shard_map/jit(_solve_triangular)/triangular_solve | solution.py:112
  (242 shorter events, 107.4 us)
Async XLA Ops:
  6.5 146.8 %all-gather.2.cloned.1.call-start = ((), (), s32[]{:S(2)}) async-start(), calls=%async_computation.2 | async-start | bytes 2949120 | tf_op jit(solution)/shard_map/all_gather | solution.py:66
  7.3 212.5 %reduce-scatter.7.cloned.1.call-start = ((), (), s32[]{:S(2)}) async-start(), calls=%async_computation.4 | async-start | bytes 983040
  7.3 34.1 %collective-permute-start = (bf16[384,768]{1,0:T(8,128)(2,1)}, bf16[384,768]{1,0:T(8,128)(2,1)S(1)}, u32[]{:S(2)}, u32[]{:S(2)}) collective-permute-start(bf16[384,768]{1,0:T(8,128)(2,1)} %param.4), channel_id=1, source_target_pairs={{0,4},{4,8},{8,12},{12,16},{16,20},{20,24},{24,28},{28,0},{1,5},{5... | collective-permute-start | bytes 1769480 | tf_op jit(solution)/shard_map/ppermute | solution.py:18
  11.7 24.2 %collective-permute-start.1 = (bf16[384]{0:T(512)(128)(2,1)S(1)}, bf16[384]{0:T(512)(128)(2,1)S(1)}, u32[]{:S(2)}, u32[]{:S(2)}) collective-permute-start(bf16[384]{0:T(512)(128)(2,1)S(1)} %get-tuple-element.33), channel_id=1, source_target_pairs={{0,4},{4,8},{8,12},{12,16},{16,20},{20,24},{24,28},{28,0},{1,5},{5... | collective-permute-start | bytes 2312 | tf_op jit(solution)/shard_map/ppermute | solution.py:18
  13.2 25.1 %collective-permute-start.9 = (bf16[384]{0:T(512)(128)(2,1)S(1)}, bf16[384]{0:T(512)(128)(2,1)S(1)}, u32[]{:S(2)}, u32[]{:S(2)}) collective-permute-start(bf16[384]{0:T(512)(128)(2,1)S(1)} %get-tuple-element.33), channel_id=1, source_target_pairs={{0,28},{4,0},{8,4},{12,8},{16,12},{20,16},{24,20},{28,24},{1,29},{... | collective-permute-start | bytes 2312 | tf_op jit(solution)/shard_map/ppermute | solution.py:18
  16.4 25.0 %collective-permute-start.8 = (bf16[384,768]{1,0:T(8,128)(2,1)}, bf16[384,768]{1,0:T(8,128)(2,1)S(1)}, u32[]{:S(2)}, u32[]{:S(2)}) collective-permute-start(bf16[384,768]{1,0:T(8,128)(2,1)} %param.4), channel_id=1, source_target_pairs={{0,28},{4,0},{8,4},{12,8},{16,12},{20,16},{24,20},{28,24},{1,29},{... | collective-permute-start | bytes 1769480 | tf_op jit(solution)/shard_map/ppermute | solution.py:18
  35.9 55.0 %collective-permute-start.3 = (bf16[384]{0:T(512)(128)(2,1)S(1)}, bf16[384]{0:T(512)(128)(2,1)S(1)}, u32[]{:S(2)}, u32[]{:S(2)}) collective-permute-start(bf16[384]{0:T(512)(128)(2,1)S(1)} %collective-permute-done.1), channel_id=1, source_target_pairs={{0,4},{4,8},{8,12},{12,16},{16,20},{20,24},{24,28},{28,0},{1,5},{5... | collective-permute-start | bytes 2312 | tf_op jit(solution)/shard_map/ppermute | solution.py:18
  38.3 52.6 %collective-permute-start.11 = (bf16[384]{0:T(512)(128)(2,1)S(1)}, bf16[384]{0:T(512)(128)(2,1)S(1)}, u32[]{:S(2)}, u32[]{:S(2)}) collective-permute-start(bf16[384]{0:T(512)(128)(2,1)S(1)} %collective-permute-done.9), channel_id=1, source_target_pairs={{0,28},{4,0},{8,4},{12,8},{16,12},{20,16},{24,20},{28,24},{1,29},{... | collective-permute-start | bytes 2312 | tf_op jit(solution)/shard_map/ppermute | solution.py:18
  41.4 54.3 %collective-permute-start.2 = (bf16[384,768]{1,0:T(8,128)(2,1)S(1)}, bf16[384,768]{1,0:T(8,128)(2,1)S(1)}, u32[]{:S(2)}, u32[]{:S(2)}) collective-permute-start(bf16[384,768]{1,0:T(8,128)(2,1)S(1)} %collective-permute-done), channel_id=1, source_target_pairs={{0,4},{4,8},{8,12},{12,16},{16,20},{20,24},{24,28},{28,0},{1,5},{5... | collective-permute-start | bytes 1769480 | tf_op jit(solution)/shard_map/ppermute | solution.py:18
  41.4 60.6 %collective-permute-start.10 = (bf16[384,768]{1,0:T(8,128)(2,1)S(1)}, bf16[384,768]{1,0:T(8,128)(2,1)S(1)}, u32[]{:S(2)}, u32[]{:S(2)}) collective-permute-start(bf16[384,768]{1,0:T(8,128)(2,1)S(1)} %collective-permute-done.8), channel_id=1, source_target_pairs={{0,28},{4,0},{8,4},{12,8},{16,12},{20,16},{24,20},{28,24},{1,29},{... | collective-permute-start | bytes 1769480 | tf_op jit(solution)/shard_map/ppermute | solution.py:18
  95.7 25.4 %collective-permute-start.4 = (bf16[384,768]{1,0:T(8,128)(2,1)S(1)}, bf16[384,768]{1,0:T(8,128)(2,1)S(1)}, u32[]{:S(2)}, u32[]{:S(2)}) collective-permute-start(bf16[384,768]{1,0:T(8,128)(2,1)S(1)} %collective-permute-done.2), channel_id=1, source_target_pairs={{0,4},{4,8},{8,12},{12,16},{16,20},{20,24},{24,28},{28,0},{1,5},{5... | collective-permute-start | bytes 1769480 | tf_op jit(solution)/shard_map/ppermute | solution.py:18
  97.2 21.7 %collective-permute-start.7 = (bf16[384]{0:T(512)(128)(2,1)S(1)}, bf16[384]{0:T(512)(128)(2,1)S(1)}, u32[]{:S(2)}, u32[]{:S(2)}) collective-permute-start(bf16[384]{0:T(512)(128)(2,1)S(1)} %collective-permute-done.5), channel_id=1, source_target_pairs={{0,4},{4,8},{8,12},{12,16},{16,20},{20,24},{24,28},{28,0},{1,5},{5... | collective-permute-start | bytes 2312 | tf_op jit(solution)/shard_map/ppermute | solution.py:18
  97.2 22.3 %collective-permute-start.15 = (bf16[384]{0:T(512)(128)(2,1)S(1)}, bf16[384]{0:T(512)(128)(2,1)S(1)}, u32[]{:S(2)}, u32[]{:S(2)}) collective-permute-start(bf16[384]{0:T(512)(128)(2,1)S(1)} %collective-permute-done.13), channel_id=1, source_target_pairs={{0,28},{4,0},{8,4},{12,8},{16,12},{20,16},{24,20},{28,24},{1,29},{... | collective-permute-start | bytes 2312 | tf_op jit(solution)/shard_map/ppermute | solution.py:18
  101.9 34.5 %collective-permute-start.12 = (bf16[384,768]{1,0:T(8,128)(2,1)S(1)}, bf16[384,768]{1,0:T(8,128)(2,1)S(1)}, u32[]{:S(2)}, u32[]{:S(2)}) collective-permute-start(bf16[384,768]{1,0:T(8,128)(2,1)S(1)} %collective-permute-done.10), channel_id=1, source_target_pairs={{0,28},{4,0},{8,4},{12,8},{16,12},{20,16},{24,20},{28,24},{1,29},{... | collective-permute-start | bytes 1769480 | tf_op jit(solution)/shard_map/ppermute | solution.py:18
  121.1 24.9 %collective-permute-start.6 = (bf16[384,768]{1,0:T(8,128)(2,1)S(1)}, bf16[384,768]{1,0:T(8,128)(2,1)S(1)}, u32[]{:S(2)}, u32[]{:S(2)}) collective-permute-start(bf16[384,768]{1,0:T(8,128)(2,1)S(1)} %collective-permute-done.4), channel_id=1, source_target_pairs={{0,4},{4,8},{8,12},{12,16},{16,20},{20,24},{24,28},{28,0},{1,5},{5... | collective-permute-start | bytes 1769480 | tf_op jit(solution)/shard_map/ppermute | solution.py:18
  136.4 15.3 %collective-permute-start.14 = (bf16[384,768]{1,0:T(8,128)(2,1)S(1)}, bf16[384,768]{1,0:T(8,128)(2,1)S(1)}, u32[]{:S(2)}, u32[]{:S(2)}) collective-permute-start(bf16[384,768]{1,0:T(8,128)(2,1)S(1)} %collective-permute-done.12), channel_id=1, source_target_pairs={{0,28},{4,0},{8,4},{12,8},{16,12},{20,16},{24,20},{28,24},{1,29},{... | collective-permute-start | bytes 1769480 | tf_op jit(solution)/shard_map/ppermute | solution.py:18
  160.5 34.5 %collective-permute-start.16 = (f32[1,384]{1,0:T(1,128)}, f32[1,384]{1,0:T(1,128)}, u32[]{:S(2)}, u32[]{:S(2)}) collective-permute-start(f32[1,384]{1,0:T(1,128)} %broadcast_in_dim.20), channel_id=1, source_target_pairs={{0,28},{4,0},{8,4},{12,8},{16,12},{20,16},{24,20},{28,24},{1,29},{... | collective-permute-start | bytes 4616 | tf_op jit(solution)/shard_map/ppermute | solution.py:18
  167.5 32.9 %collective-permute-start.20 = (f32[1,384]{1,0:T(1,128)}, f32[1,384]{1,0:T(1,128)}, u32[]{:S(2)}, u32[]{:S(2)}) collective-permute-start(f32[1,384]{1,0:T(1,128)} %broadcast_in_dim.24), channel_id=1, source_target_pairs={{0,4},{4,8},{8,12},{12,16},{16,20},{20,24},{24,28},{28,0},{1,5},{5... | collective-permute-start | bytes 4616 | tf_op jit(solution)/shard_map/ppermute | solution.py:18
  195.0 91.0 %reduce-scatter.5.cloned.1.call-start = ((), (), s32[]{:S(2)}) async-start(), calls=%async_computation.3 | async-start | bytes 491520 | tf_op jit(solution)/shard_map/reduce_scatter | solution.py:59
  208.0 12.8 %collective-permute-start.19 = (f32[1,384]{1,0:T(1,128)S(1)}, f32[1,384]{1,0:T(1,128)S(1)}, u32[]{:S(2)}, u32[]{:S(2)}) collective-permute-start(f32[1,384]{1,0:T(1,128)S(1)} %reshape_add_fusion.3), channel_id=1, source_target_pairs={{0,28},{4,0},{8,4},{12,8},{16,12},{20,16},{24,20},{28,24},{1,29},{... | collective-permute-start | bytes 4616 | tf_op jit(solution)/shard_map/ppermute | solution.py:18
  226.6 11.2 %collective-permute-start.24 = (bf16[64,384]{1,0:T(8,128)(2,1)S(1)}, bf16[64,384]{1,0:T(8,128)(2,1)S(1)}, u32[]{:S(2)}, u32[]{:S(2)}) collective-permute-start(bf16[64,384]{1,0:T(8,128)(2,1)S(1)} %multiply_convert_fusion), channel_id=1, source_target_pairs={{0,4},{4,8},{8,12},{12,16},{16,20},{20,24},{24,28},{28,0},{1,5},{5... | collective-permute-start | bytes 147464 | tf_op jit(solution)/shard_map/ppermute | solution.py:18
  234.9 15.3 %collective-permute-start.32 = (f32[64,384]{1,0:T(8,128)S(1)}, f32[64,384]{1,0:T(8,128)S(1)}, u32[]{:S(2)}, u32[]{:S(2)}) collective-permute-start(f32[64,384]{1,0:T(8,128)S(1)} %fusion.18), channel_id=1, source_target_pairs={{0,28},{4,0},{8,4},{12,8},{16,12},{20,16},{24,20},{28,24},{1,29},{... | collective-permute-start | bytes 294920 | tf_op jit(solution)/shard_map/ppermute | solution.py:18
  236.8 24.6 %collective-permute-start.36 = (f32[64,384]{1,0:T(8,128)S(1)}, f32[64,384]{1,0:T(8,128)S(1)}, u32[]{:S(2)}, u32[]{:S(2)}) collective-permute-start(f32[64,384]{1,0:T(8,128)S(1)} %fusion.6), channel_id=1, source_target_pairs={{0,4},{4,8},{8,12},{12,16},{16,20},{20,24},{24,28},{28,0},{1,5},{5... | collective-permute-start | bytes 294920 | tf_op jit(solution)/shard_map/ppermute | solution.py:18
  250.5 14.2 %collective-permute-start.33 = (f32[64,384]{1,0:T(8,128)S(1)}, f32[64,384]{1,0:T(8,128)S(1)}, u32[]{:S(2)}, u32[]{:S(2)}) collective-permute-start(f32[64,384]{1,0:T(8,128)S(1)} %convolution_add_fusion.8), channel_id=1, source_target_pairs={{0,28},{4,0},{8,4},{12,8},{16,12},{20,16},{24,20},{28,24},{1,29},{... | collective-permute-start | bytes 294920 | tf_op jit(solution)/shard_map/ppermute | solution.py:18
  (68 other events, 627.6 us)
Sparse Core Ops, SparseCore 0:
  8.9 26.7 all-gather.1
  195.1 24.6 reduce-scatter.6
  261.5 20.3 reduce-scatter.4
where the time goes:
time: 345 us; the launch traced here: 344 us
  starting transfers between devices  80.1 us (23%)
  waiting for transfers between devices  80 us (23%)
  other arithmetic  73.4 us (21%)
  matrix products  47.9 us (14%)
  blocking collectives  42.7 us (12%)
  between operations  13.9 us (4%)
  local copies, waits for them, and re-layouts  5.8 us (2%)
    ppermute x40, starting transfers between devices, shifted(): return lax.ppermute(value, axis, pairs)  80 us
    ppermute x40, waiting for transfers between devices, shifted(): return lax.ppermute(value, axis, pairs)  73.2 us
    reduce_sum x1, other arithmetic, pair_weights(): jnp.sum((lists_here[:, :, None] == positions[None, None, :]).astype(jnp.f...  44.8 us
    psum x1, blocking collectives, local(): gram = lax.psum(partial_gram, ('blk', 'sub'))  37 us
    dot_general x9, matrix products, pair_weights(): lax.dot_general(block_feats, moving_feats, (((1,), (1,)), ((), ())), pref...  33.6 us
    dot_general x9, matrix products, product_work(): col_term = jnp.dot(block_eigen, tile, preferred_element_type=jnp.float32)  8.03 us
  transfers between devices with their start and end apart: 43, of which 19 were waited for; matrix products, arithmetic and copies ran while one was open for 30% of the time, Pallas kernels for 0%

commit v1 on v0

v1 whole, which is shorter than its diff:
```python
import functools
import math

import jax
import jax.numpy as jnp
from jax import lax
from jax.experimental import pallas as pl
from jax.experimental.pallas import tpu as pltpu
from jax.sharding import PartitionSpec as P

NT = (((1,), (1,)), ((), ()))
LANES = 128
GROUP = 32
CHUNK = 256
MESH = pl.DeviceIdType.MESH


def ring_place(blk, count, folded):
    if not folded:
        return blk
    return jnp.where(blk % 2 == 0, blk // 2, count - 1 - blk // 2)


def ring_block(place, count, folded):
    if not folded:
        return place
    return jnp.where(place < count // 2, 2 * place, 2 * (count - 1 - place) + 1)


def kernel(
    blks, subs, half, feat_dim,
    feats, lists, scale_rows, eigen,
    mixed_out, gram_out,
    block_feats, moving, lists_in, scales_in, own_words, their_words, weight_tiles, half_norms,
    row_deg, deg_send, deg_recv, low_own, block_low, moving_low,
    term_send, term_recv, gram_send_a, gram_a, gram_send_b, gram_b,
    s_feat, r_feat, s_ring, r_ring, s_list, r_list, s_scale, r_scale,
    s_deg, r_deg, s_low, r_low, s_term, r_term, s_gram, r_gram,
):
    rows = feats.shape[0]
    block = rows * subs
    folded = blks == 2 * half
    blk = lax.axis_index("blk")
    sub = lax.axis_index("sub")
    place = ring_place(blk, blks, folded)
    ahead = [ring_block((place + d) % blks, blks, folded) for d in range(half + 1)]
    behind = [ring_block((place + blks - d) % blks, blks, folded) for d in range(half + 1)]
    peers = [(sub + k) % subs for k in range(subs)]
    twice = [(blk - behind[d] + blks) % blks == half for d in range(half + 1)]
    both = [d for d in range(1, half + 1) if not (folded and d == half)]

    barrier = pltpu.get_barrier_semaphore()
    for k in range(1, blks):
        pl.semaphore_signal(barrier, inc=1, device_id={"blk": (blk + k) % blks}, device_id_type=MESH)
    for k in range(1, subs):
        pl.semaphore_signal(barrier, inc=1, device_id={"sub": peers[k]}, device_id_type=MESH)
    pl.semaphore_wait(barrier, blks - 1 + subs - 1)

    def send(src, dst, ssem, rsem, where):
        copy = pltpu.make_async_remote_copy(
            src_ref=src, dst_ref=dst, send_sem=ssem, recv_sem=rsem,
            device_id=where, device_id_type=MESH,
        )
        copy.start()
        return copy

    def span(index):
        return pl.ds(pl.multiple_of(index * rows, rows), rows)

    ring = [send(feats, moving.at[0], s_ring.at[0], r_ring.at[0], {"blk": ahead[1]})]
    gathers = [
        send(feats, block_feats.at[span(sub), :], s_feat.at[k - 1], r_feat.at[k - 1], {"sub": peers[k]})
        for k in range(1, subs)
    ]
    small = []
    for d in range(1, half + 1):
        small.append(send(
            scale_rows.at[:, span(sub)], scales_in.at[d - 1],
            s_scale.at[d - 1], r_scale.at[d - 1], {"blk": ahead[d]},
        ))
    for d in both:
        j = (blk - ahead[d] + blks + half) % blks
        small.append(send(
            lists.at[j, :, span(sub)], lists_in.at[d - 1, 0],
            s_list.at[d - 1, 0], r_list.at[d - 1, 0], {"blk": ahead[d]},
        ))
        if folded:
            small.append(send(
                lists.at[2 * half, :, span(sub)], lists_in.at[d - 1, 1],
                s_list.at[d - 1, 1], r_list.at[d - 1, 1], {"blk": ahead[d]},
            ))
    block_feats[span(sub), :] = feats[...]

    def words_of(j):
        listed = lists[j] - sub * rows
        inside = jnp.logical_and(listed >= 0, listed < rows)
        one = jnp.ones_like(listed)
        bits = jnp.where(inside, jnp.left_shift(one, jnp.right_shift(listed, 4) & 30), 0)
        low = listed & (GROUP - 1)
        spot = lax.broadcasted_iota(jnp.int32, (GROUP, block), 0)
        total = jnp.zeros((GROUP, block), jnp.int32)
        for m in range(listed.shape[0]):
            total = total + jnp.where(low[m : m + 1, :] == spot, bits[m : m + 1, :], 0)
        return total

    for d in range(half + 1):
        own_words[d] = words_of((blk - behind[d] + blks + half) % blks)
        if folded and d > 0:
            @pl.when(twice[d])
            def _():
                own_words[d] = own_words[d] + words_of(2 * half)

    def norm_rows(c, carry):
        at = pl.ds(pl.multiple_of(c * CHUNK, CHUNK), CHUNK)
        part = block_feats[at, :].astype(jnp.float32)
        half_norms[:, at] = lax.dot_general(
            jnp.full((8, part.shape[1]), 0.5, jnp.float32), part * part, NT,
            precision=lax.Precision.HIGHEST, preferred_element_type=jnp.float32,
        )
        return carry

    def tile(d, source):
        values = source[...]
        wide = values.astype(jnp.float32)
        norm_q = 0.5 * jnp.sum(wide * wide, axis=1, keepdims=True)
        scale_q = scale_rows[:, span(sub)] if d == 0 else scales_in[d - 1]
        rate_q = (2.0 / feat_dim) / jnp.transpose(scale_q)[:, :1]
        if d in both:
            def their_of(which):
                listed = jnp.transpose(lists_in[d - 1, which])
                bits = jnp.left_shift(jnp.ones_like(listed), 2 * jnp.right_shift(listed, 7))
                low = listed & (LANES - 1)
                spot = lax.broadcasted_iota(jnp.int32, (rows, LANES), 1)
                words = jnp.zeros((rows, LANES), jnp.int32)
                for m in range(listed.shape[1]):
                    words = words + jnp.where(low[:, m : m + 1] == spot, bits[:, m : m + 1], 0)
                return words

            their_words[...] = their_of(0)
            if folded:
                @pl.when(twice[d])
                def _():
                    their_words[...] = their_words[...] + their_of(1)

        def step(c, col_total):
            at = pl.ds(pl.multiple_of(c * CHUNK, CHUNK), CHUNK)
            inner = lax.dot_general(
                source[...], block_feats[at, :], NT, preferred_element_type=jnp.float32
            )
            rate_p = 1.0 / scale_rows[0:1, at]
            affinity = jnp.exp((inner - half_norms[0:1, at] - norm_q) * (rate_q * rate_p))
            groups = 2 * lax.broadcasted_iota(jnp.int32, (rows // GROUP, GROUP, CHUNK), 0)
            count = jnp.right_shift(own_words[d, :, at][None], groups) & 3
            count = count.reshape(rows, CHUNK)
            if d in both:
                base = c * (CHUNK // LANES)
                their = their_words[...]
                count = count + jnp.concatenate(
                    [jnp.right_shift(their, 2 * (base + i)) & 3 for i in range(CHUNK // LANES)], axis=1
                )
            weight = affinity * count.astype(jnp.float32)
            weight_tiles[d, :, at] = weight.astype(jnp.bfloat16)
            down = jnp.sum(weight, axis=0, keepdims=True)
            row_deg[0:1, at] = down if d == 0 else row_deg[0:1, at] + down
            for i in range(CHUNK // LANES):
                col_total = col_total + weight[:, i * LANES : (i + 1) * LANES]
            return col_total

        col_total = lax.fori_loop(
            0, block // CHUNK, step, jnp.zeros((rows, LANES), jnp.float32)
        )
        return jnp.sum(jnp.transpose(col_total), axis=0, keepdims=True)

    def advance(d):
        ring[d - 1].wait_recv()
        if d < half:
            ring.append(send(
                moving.at[d - 1], moving.at[d], s_ring.at[d], r_ring.at[d], {"blk": ahead[1]}
            ))

    advance(1)
    for copy in gathers:
        copy.wait_recv()
    lax.fori_loop(0, block // CHUNK, norm_rows, 0)
    for copy in small:
        copy.wait_recv()
    own_col = tile(0, feats)

    exchanges = []
    for d in range(1, half + 1):
        if d > 1:
            advance(d)
        col = tile(d, moving.at[d - 1])
        deg_send[d - 1] = jnp.broadcast_to(col, (8, rows))
        exchanges.append(send(
            deg_send.at[d - 1], deg_recv.at[d - 1], s_deg.at[d - 1], r_deg.at[d - 1],
            {"blk": behind[d]},
        ))
    for k in range(1, subs):
        slot = half + k - 1
        deg_send[slot] = jnp.broadcast_to(row_deg[0:1, span(peers[k])], (8, rows))
        exchanges.append(send(
            deg_send.at[slot], deg_recv.at[slot], s_deg.at[slot], r_deg.at[slot],
            {"sub": peers[k]},
        ))
    total = own_col + row_deg[0:1, span(sub)]
    for slot, copy in enumerate(exchanges):
        copy.wait_recv()
        total = total + deg_recv[slot, 0:1, :]
    inv_root = lax.rsqrt(1.0 + 0.5 * total)
    scaled = eigen[...] * inv_root
    low_own[...] = scaled.astype(jnp.bfloat16)

    lows = []
    for d in range(1, half + 1):
        lows.append(send(
            low_own, moving_low.at[d - 1], s_low.at[d - 1], r_low.at[d - 1], {"blk": ahead[d]}
        ))
    for k in range(1, subs):
        slot = half + k - 1
        lows.append(send(
            low_own, block_low.at[sub], s_low.at[slot], r_low.at[slot], {"sub": peers[k]}
        ))
    block_low[sub] = low_own[...]
    for k in range(1, subs):
        lows[half + k - 1].wait_recv()

    def col_term(d):
        acc = None
        for k in range(subs):
            part = lax.dot_general(
                block_low[k], weight_tiles[d, :, k * rows : (k + 1) * rows], NT,
                preferred_element_type=jnp.float32,
            )
            acc = part if acc is None else acc + part
        return acc

    terms = []
    for d in range(1, half + 1):
        term_send[d - 1] = col_term(d)
        terms.append(send(
            term_send.at[d - 1], term_recv.at[d - 1], s_term.at[d - 1], r_term.at[d - 1],
            {"blk": behind[d]},
        ))
    for d in range(1, half + 1):
        lows[d - 1].wait_recv()

    def row_term(index):
        acc = jnp.dot(low_own[...], weight_tiles[0, :, span(index)], preferred_element_type=jnp.float32)
        for d in range(1, half + 1):
            acc = acc + jnp.dot(
                moving_low[d - 1], weight_tiles[d, :, span(index)], preferred_element_type=jnp.float32
            )
        return acc

    for k in range(1, subs):
        slot = half + k - 1
        term_send[slot] = row_term(peers[k])
        terms.append(send(
            term_send.at[slot], term_recv.at[slot], s_term.at[slot], r_term.at[slot],
            {"sub": peers[k]},
        ))
    side = row_term(sub) + col_term(0)
    for slot, copy in enumerate(terms):
        copy.wait_recv()
        side = side + term_recv[slot]
    mixed = inv_root * (scaled + 0.5 * side)
    mixed_out[...] = mixed
    gram = lax.dot_general(
        mixed, mixed, NT, precision=lax.Precision.HIGHEST, preferred_element_type=jnp.float32
    )

    grams = []
    gram_send_a[...] = gram
    for k in range(1, subs):
        grams.append(send(
            gram_send_a, gram_a.at[k - 1], s_gram.at[k - 1], r_gram.at[k - 1], {"sub": peers[k]}
        ))
    for k in range(1, subs):
        grams[k - 1].wait_recv()
        gram = gram + gram_a[k - 1]
    gram_send_b[...] = gram
    for k in range(1, blks):
        slot = subs - 1 + k - 1
        grams.append(send(
            gram_send_b, gram_b.at[k - 1], s_gram.at[slot], r_gram.at[slot],
            {"blk": (blk + k) % blks},
        ))
    for k in range(1, blks):
        grams[subs - 1 + k - 1].wait_recv()
        gram = gram + gram_b[k - 1]
    gram_out[...] = gram
    for copy in ring + gathers + small + exchanges + lows + terms + grams:
        copy.wait_send()


def local(blks, subs, features, scales, neighbor_lists, eigen_block):
    rows, feat_dim = features.shape
    half = (neighbor_lists.shape[0] - 1) // 2
    block = neighbor_lists.shape[2]
    members = neighbor_lists.shape[1]
    eig = eigen_block.shape[0]
    links = half + subs - 1
    scale_rows = jnp.broadcast_to(scales.astype(jnp.float32)[None, :], (8, block))
    dma = pltpu.SemaphoreType.DMA
    here = pl.BlockSpec(memory_space=pltpu.VMEM)
    f32, bf16, i32 = jnp.float32, jnp.bfloat16, jnp.int32
    mixed, gram = pl.pallas_call(
        functools.partial(kernel, blks, subs, half, feat_dim),
        out_shape=(
            jax.ShapeDtypeStruct((eig, rows), f32),
            jax.ShapeDtypeStruct((eig, eig), f32),
        ),
        in_specs=[here] * 4,
        out_specs=(here, here),
        scratch_shapes=[
            pltpu.VMEM((block, feat_dim), bf16),
            pltpu.VMEM((half, rows, feat_dim), bf16),
            pltpu.VMEM((half, 2, members, rows), i32),
            pltpu.VMEM((half, 8, rows), f32),
            pltpu.VMEM((half + 1, GROUP, block), i32),
            pltpu.VMEM((rows, LANES), i32),
            pltpu.VMEM((half + 1, rows, block), bf16),
            pltpu.VMEM((8, block), f32),
            pltpu.VMEM((8, block), f32),
            pltpu.VMEM((links, 8, rows), f32),
            pltpu.VMEM((links, 8, rows), f32),
            pltpu.VMEM((eig, rows), bf16),
            pltpu.VMEM((subs, eig, rows), bf16),
            pltpu.VMEM((half, eig, rows), bf16),
            pltpu.VMEM((links, eig, rows), f32),
            pltpu.VMEM((links, eig, rows), f32),
            pltpu.VMEM((eig, eig), f32),
            pltpu.VMEM((subs - 1, eig, eig), f32),
            pltpu.VMEM((eig, eig), f32),
            pltpu.VMEM((blks - 1, eig, eig), f32),
            dma((subs - 1,)), dma((subs - 1,)),
            dma((half,)), dma((half,)),
            dma((half, 2)), dma((half, 2)),
            dma((half,)), dma((half,)),
            dma((links,)), dma((links,)),
            dma((links,)), dma((links,)),
            dma((links,)), dma((links,)),
            dma((subs + blks - 2,)), dma((subs + blks - 2,)),
        ],
        compiler_params=pltpu.CompilerParams(
            collective_id=0, has_side_effects=True, vmem_limit_bytes=56 * 1024 * 1024
        ),
    )(features, neighbor_lists_of(neighbor_lists), scale_rows, eigen_block)
    lower = jnp.linalg.cholesky(gram)
    total_rows = rows * blks * subs
    return math.sqrt(total_rows) * jax.scipy.linalg.solve_triangular(lower, mixed, lower=True)


def neighbor_lists_of(neighbor_lists):
    return neighbor_lists.astype(jnp.int32)


def solution(mesh):
    placed = (P(("blk", "sub"), None), P("blk"), P(None, None, "blk"), P(None, ("blk", "sub")))
    return jax.shard_map(
        functools.partial(local, mesh.shape["blk"], mesh.shape["sub"]),
        mesh=mesh, in_specs=placed, out_specs=P(None, ("blk", "sub")), check_vma=False,
    )
```

time: 345 us -> 122 us (0.35)
  Pallas kernels: 0 us -> 106 us
  starting transfers between devices: 80.1 us -> 0 us
  waiting for transfers between devices: 80 us -> 0 us
  other arithmetic: 73.4 us -> 12.1 us
  matrix products: 47.9 us -> 0.93 us
  blocking collectives: 42.7 us -> 0 us
  between operations: 13.9 us -> 0.06 us
  local copies, waits for them, and re-layouts: 5.8 us -> 2.22 us
    pallas_call x0 -> x1, Pallas kernels: none -> 106 us  [local(): pl.pallas_call(functools.partial(kernel, blks, subs, half, feat_dim), out...]
    ppermute x40 -> x0, starting transfers between devices: 80 us -> none  [shifted(): return lax.ppermute(value, axis, pairs)]
    ppermute x40 -> x0, waiting for transfers between devices: 73.2 us -> none  [shifted(): return lax.ppermute(value, axis, pairs)]
    reduce_sum x11 -> x0, other arithmetic: 52.9 us -> none  [the longest x1 44.8 us: pair_weights(): jnp.sum((lists_here[:, :, None] == positions[None, None, :]).astype(jnp.f...]
    dot_general x28 -> x0, matrix products: 47 us -> none  [the longest x9 33.6 us: pair_weights(): lax.dot_general(block_feats, moving_feats, (((1,), (1,)), ((), ())), pref...]
    psum x1 -> x0, blocking collectives: 37 us -> none  [local(): gram = lax.psum(partial_gram, ('blk', 'sub'))]
    unnamed x4 -> x0, waiting for transfers between devices: 6.85 us -> none
    convert_element_type x10 -> x0, other arithmetic: 5.98 us -> none  [the longest x9 5.97 us: pair_weights(): moving_scales.astype(jnp.float32)[None, :]]
  transfers between devices with their start and end apart: 43 -> 0, of which waited for: 19 -> 0; matrix products, arithmetic and copies ran while one was open for 30% -> 0% of each run, Pallas kernels for 0% -> 0%
where the time goes in v1:
time: 122 us; the launch traced here: 121 us
  Pallas kernels  106 us (87%)
  other arithmetic  12.1 us (10%)
  local copies, waits for them, and re-layouts  2.22 us (2%)
    pallas_call x1, Pallas kernels, local(): pl.pallas_call(functools.partial(kernel, blks, subs, half, feat_dim), out...  106 us
    another operation x3, other arithmetic, local(): lower = jnp.linalg.cholesky(gram)  6.52 us
    another operation x2, other arithmetic, local(): jax.scipy.linalg.solve_triangular(lower, mixed, lower=True)  5.55 us

profile of v1, /device:TPU:0, one launch (start us, length us, event | category | flops | bytes accessed | tf_op | source)
XLA Modules:
  0.0 120.9 jit_solution(15136322418427852673)
XLA Ops:
  0.0 1.3 %broadcast_in_dim.3.scale_rows = f32[8,1536]{1,0:T(8,128)} broadcast(bf16[1536]{0:T(1024)(128)(2,1)} %param.5), dimensions={1} | broadcast | bytes 52224 | tf_op jit(solution)/shard_map/broadcast_in_dim | solution.py:304
  1.3 105.6 %shard_map.46 = (f32[64,384]{1,0:T(8,128)}, f32[64,64]{1,0:T(8,128)}) custom-call(bf16[384,768]{1,0:T(8,128)(2,1)} %feats.1, s32[9,16,1536]{2,1,0:T(8,128)} %lists.1, f32[8,1536]{1,0:T(8,128)} %broadcast_in_dim.3.scale_rows, f32[64,384]{1,0:T(8,128)} %eigen.1), custom_call_target="tpu_custom_call" | custom-call | tf_op jit(solution)/shard_map/pallas_call | solution.py:308
  106.9 0.0 copy-start
  106.9 0.9 copy.5
  107.8 0.0 copy-done
  107.8 0.0 copy-start.1
  107.9 5.8 %cholesky.16 = f32[64,64]{1,0:T(8,128)S(1)} custom-call(f32[64,64]{1,0:T(8,128)S(1)} %fusion.2), custom_call_target="Cholesky" | custom-call | tf_op jit(solution)/shard_map/jit(cholesky)/cholesky | solution.py:350
  113.7 0.6 compare_reduce_fusion
  114.4 0.7 fusion
  115.0 4.9 %custom-call.7 = f32[1,64,64]{1,2,0:T(8,128)S(1)} custom-call(f32[1,64,64]{2,1,0:T(8,128)S(1)} %fusion), custom_call_target="InvertDiagBlocksLowerTriangular" | custom-call | tf_op jit(solution)/shard_map/jit(_solve_triangular)/triangular_solve | solution.py:352
  119.9 0.0 copy-done.1
  120.0 0.9 convolution_multiply_fusion
  (2 shorter events, 0.0 us)
Async XLA Ops:
  106.9 0.9 copy-start
  107.8 12.1 %copy-start.1 = (f32[64,384]{1,0:T(8,128)S(1)}, f32[64,384]{1,0:T(8,128)}, u32[]{:S(2)}) copy-start(f32[64,384]{1,0:T(8,128)} %get-tuple-element.8) | copy-start | bytes 294916

commit v2 on v1

--- a/solution.py
+++ b/solution.py
@@ -30,7 +30,7 @@
 def kernel(
     blks, subs, half, feat_dim,
     feats, lists, scale_rows, eigen,
-    mixed_out, gram_out,
+    mixed_out, inverse_out,
     block_feats, moving, lists_in, scales_in, own_words, their_words, weight_tiles, half_norms,
     row_deg, deg_send, deg_recv, low_own, block_low, moving_low,
     term_send, term_recv, gram_send_a, gram_a, gram_send_b, gram_b,
@@ -289,7 +289,19 @@
     for k in range(1, blks):
         grams[subs - 1 + k - 1].wait_recv()
         gram = gram + gram_b[k - 1]
-    gram_out[...] = gram
+    eig = gram.shape[0]
+    spot_row = lax.broadcasted_iota(jnp.int32, (eig, eig), 0)
+    spot_col = lax.broadcasted_iota(jnp.int32, (eig, eig), 1)
+    both_parts = jnp.concatenate([gram, (spot_row == spot_col).astype(jnp.float32)], axis=1)
+    below = lax.broadcasted_iota(jnp.int32, (eig, 1), 0)
+    roots = jnp.zeros((eig, 1), jnp.float32)
+    for j in range(eig):
+        pivot = both_parts[j : j + 1, j : j + 1]
+        roots = jnp.where(below == j, lax.rsqrt(pivot), roots)
+        if j + 1 < eig:
+            factor = jnp.where(below > j, both_parts[:, j : j + 1], 0.0)
+            both_parts = both_parts - factor * (both_parts[j : j + 1, :] * (1.0 / pivot))
+    inverse_out[...] = both_parts[:, eig:] * (roots * math.sqrt(rows * subs * blks))
     for copy in ring + gathers + small + exchanges + lows + terms + grams:
         copy.wait_send()
 
@@ -305,7 +317,7 @@
     dma = pltpu.SemaphoreType.DMA
     here = pl.BlockSpec(memory_space=pltpu.VMEM)
     f32, bf16, i32 = jnp.float32, jnp.bfloat16, jnp.int32
-    mixed, gram = pl.pallas_call(
+    mixed, inverse = pl.pallas_call(
         functools.partial(kernel, blks, subs, half, feat_dim),
         out_shape=(
             jax.ShapeDtypeStruct((eig, rows), f32),
@@ -347,9 +359,9 @@
             collective_id=0, has_side_effects=True, vmem_limit_bytes=56 * 1024 * 1024
         ),
     )(features, neighbor_lists_of(neighbor_lists), scale_rows, eigen_block)
-    lower = jnp.linalg.cholesky(gram)
-    total_rows = rows * blks * subs
-    return math.sqrt(total_rows) * jax.scipy.linalg.solve_triangular(lower, mixed, lower=True)
+    return jnp.dot(
+        inverse, mixed, precision=lax.Precision.HIGHEST, preferred_element_type=jnp.float32
+    )
 
 
 def neighbor_lists_of(neighbor_lists):

time: 122 us -> 115 us (0.943)
  other arithmetic: 12.1 us -> 0 us
  Pallas kernels: 106 us -> 111 us
    another operation x5 -> x0, other arithmetic: 12.1 us -> none  [the longest x3 6.52 us: local(): lower = jnp.linalg.cholesky(gram)]
    pallas_call x1, Pallas kernels: 106 us -> 111 us  [local(): pl.pallas_call(functools.partial(kernel, blks, subs, half, feat_dim), out...]
    dot_general x0 -> x1, matrix products: none -> 1.77 us  [local(): jnp.dot(inverse, mixed, precision=lax.Precision.HIGHEST, preferred_elemen...]
where the time goes in v2:
time: 115 us; the launch traced here: 114 us
  Pallas kernels  111 us (97%)
  matrix products  1.77 us (2%)
  local copies, waits for them, and re-layouts  1.31 us (1%)
    pallas_call x1, Pallas kernels, local(): pl.pallas_call(functools.partial(kernel, blks, subs, half, feat_dim), out...  111 us

profile of v2, /device:TPU:0, one launch (start us, length us, event | category | flops | bytes accessed | tf_op | source)
XLA Modules:
  0.0 114.4 jit_solution(5646559191705479296)
XLA Ops:
  0.0 1.3 %broadcast_in_dim.2.scale_rows = f32[8,1536]{1,0:T(8,128)} broadcast(bf16[1536]{0:T(1024)(128)(2,1)} %param.5), dimensions={1} | broadcast | bytes 52224 | tf_op jit(solution)/shard_map/broadcast_in_dim | solution.py:316
  1.3 111.3 %shard_map.46 = (f32[64,384]{1,0:T(8,128)}, f32[64,64]{1,0:T(8,128)}) custom-call(bf16[384,768]{1,0:T(8,128)(2,1)} %feats.1, s32[9,16,1536]{2,1,0:T(8,128)} %lists.1, f32[8,1536]{1,0:T(8,128)} %broadcast_in_dim.2.scale_rows, f32[64,384]{1,0:T(8,128)} %eigen.1), custom_call_target="tpu_custom_call" | custom-call | tf_op jit(solution)/shard_map/pallas_call | solution.py:320
  112.6 1.8 %fusion = f32[64,384]{1,0:T(8,128)} fusion(f32[64,64]{1,0:T(8,128)} %get-tuple-element.7, f32[64,384]{1,0:T(8,128)} %get-tuple-element.8), kind=kOutput, calls=%fused_computation | convolution fusion | flops 18874368 | bytes 212992 | tf_op jit(solution)/shard_map/dot_general | solution.py:362

commit v3 on v2

--- a/solution.py
+++ b/solution.py
@@ -31,10 +31,10 @@
     blks, subs, half, feat_dim,
     feats, lists, scale_rows, eigen,
     mixed_out, inverse_out,
-    block_feats, moving, lists_in, scales_in, own_words, their_words, weight_tiles, half_norms,
+    block_feats, moving, back, lists_in, scales_in, own_words, their_words, weight_tiles, half_norms,
     row_deg, deg_send, deg_recv, low_own, block_low, moving_low,
-    term_send, term_recv, gram_send_a, gram_a, gram_send_b, gram_b,
-    s_feat, r_feat, s_ring, r_ring, s_list, r_list, s_scale, r_scale,
+    term_send, term_recv, gram_all, gram_send_a, gram_a, gram_send_b, gram_b, gram_send_c, gram_c,
+    s_feat, r_feat, s_ring, r_ring, s_back, r_back, s_list, r_list, s_scale, r_scale,
     s_deg, r_deg, s_low, r_low, s_term, r_term, s_gram, r_gram,
 ):
     rows = feats.shape[0]
@@ -66,6 +66,25 @@
 
     def span(index):
         return pl.ds(pl.multiple_of(index * rows, rows), rows)
+
+    near = rows // 4 if folded else rows
+    far = pl.ds(near, rows - near)
+
+    def back_send(t):
+        last = t == half
+        return send(
+            feats.at[far, :] if t == 1 else back.at[t - 2],
+            moving.at[half - 1, far, :] if last else back.at[t - 1],
+            s_back.at[t - 1], r_back.at[t - 1], {"blk": behind[1]},
+        )
+
+    backs = [back_send(1)] if folded else []
+
+    def back_advance(t):
+        if folded:
+            backs[t - 1].wait_recv()
+            if t < half:
+                backs.append(back_send(t + 1))
 
     ring = [send(feats, moving.at[0], s_ring.at[0], r_ring.at[0], {"blk": ahead[1]})]
     gathers = [
@@ -176,7 +195,11 @@
         if d < half:
             ring.append(send(
                 moving.at[d - 1], moving.at[d], s_ring.at[d], r_ring.at[d], {"blk": ahead[1]}
+            ) if d < half - 1 else send(
+                moving.at[d - 1, pl.ds(0, near), :], moving.at[d, pl.ds(0, near), :],
+                s_ring.at[d], r_ring.at[d], {"blk": ahead[1]},
             ))
+        back_advance(d)
 
     advance(1)
     for copy in gathers:
@@ -237,7 +260,7 @@
 
     terms = []
     for d in range(1, half + 1):
-        term_send[d - 1] = col_term(d)
+        term_send[d - 1] = col_term(d).astype(jnp.bfloat16)
         terms.append(send(
             term_send.at[d - 1], term_recv.at[d - 1], s_term.at[d - 1], r_term.at[d - 1],
             {"blk": behind[d]},
@@ -255,7 +278,7 @@
 
     for k in range(1, subs):
         slot = half + k - 1
-        term_send[slot] = row_term(peers[k])
+        term_send[slot] = row_term(peers[k]).astype(jnp.bfloat16)
         terms.append(send(
             term_send.at[slot], term_recv.at[slot], s_term.at[slot], r_term.at[slot],
             {"sub": peers[k]},
@@ -263,7 +286,7 @@
     side = row_term(sub) + col_term(0)
     for slot, copy in enumerate(terms):
         copy.wait_recv()
-        side = side + term_recv[slot]
+        side = side + term_recv[slot].astype(jnp.float32)
     mixed = inv_root * (scaled + 0.5 * side)
     mixed_out[...] = mixed
     gram = lax.dot_general(
@@ -271,15 +294,23 @@
     )
 
     grams = []
+    part = gram.shape[0] // subs
+
+    def piece(index):
+        return pl.ds(pl.multiple_of(index * part, part), part)
+
+    gram_all[...] = gram
     gram_send_a[...] = gram
     for k in range(1, subs):
         grams.append(send(
-            gram_send_a, gram_a.at[k - 1], s_gram.at[k - 1], r_gram.at[k - 1], {"sub": peers[k]}
-        ))
+            gram_send_a.at[piece(peers[k]), :], gram_a.at[k - 1],
+            s_gram.at[k - 1], r_gram.at[k - 1], {"sub": peers[k]},
+        ))
+    share = gram_all[piece(sub), :]
     for k in range(1, subs):
         grams[k - 1].wait_recv()
-        gram = gram + gram_a[k - 1]
-    gram_send_b[...] = gram
+        share = share + gram_a[k - 1]
+    gram_send_b[...] = share
     for k in range(1, blks):
         slot = subs - 1 + k - 1
         grams.append(send(
@@ -288,7 +319,17 @@
         ))
     for k in range(1, blks):
         grams[subs - 1 + k - 1].wait_recv()
-        gram = gram + gram_b[k - 1]
+        share = share + gram_b[k - 1]
+    gram_send_c[...] = share
+    for k in range(1, subs):
+        slot = subs - 1 + blks - 1 + k - 1
+        grams.append(send(
+            gram_send_c, gram_c.at[sub], s_gram.at[slot], r_gram.at[slot], {"sub": peers[k]}
+        ))
+    gram_c[sub] = share
+    for k in range(1, subs):
+        grams[subs - 1 + blks - 1 + k - 1].wait_recv()
+    gram = gram_c[...].reshape(subs * part, subs * part)
     eig = gram.shape[0]
     spot_row = lax.broadcasted_iota(jnp.int32, (eig, eig), 0)
     spot_col = lax.broadcasted_iota(jnp.int32, (eig, eig), 1)
@@ -302,7 +343,7 @@
             factor = jnp.where(below > j, both_parts[:, j : j + 1], 0.0)
             both_parts = both_parts - factor * (both_parts[j : j + 1, :] * (1.0 / pivot))
     inverse_out[...] = both_parts[:, eig:] * (roots * math.sqrt(rows * subs * blks))
-    for copy in ring + gathers + small + exchanges + lows + terms + grams:
+    for copy in ring + backs + gathers + small + exchanges + lows + terms + grams:
         copy.wait_send()
 
 
@@ -328,6 +369,7 @@
         scratch_shapes=[
             pltpu.VMEM((block, feat_dim), bf16),
             pltpu.VMEM((half, rows, feat_dim), bf16),
+            pltpu.VMEM((half - 1, rows - rows // 4, feat_dim), bf16),
             pltpu.VMEM((half, 2, members, rows), i32),
             pltpu.VMEM((half, 8, rows), f32),
             pltpu.VMEM((half + 1, GROUP, block), i32),
@@ -340,20 +382,24 @@
             pltpu.VMEM((eig, rows), bf16),
             pltpu.VMEM((subs, eig, rows), bf16),
             pltpu.VMEM((half, eig, rows), bf16),
-            pltpu.VMEM((links, eig, rows), f32),
-            pltpu.VMEM((links, eig, rows), f32),
+            pltpu.VMEM((links, eig, rows), bf16),
+            pltpu.VMEM((links, eig, rows), bf16),
             pltpu.VMEM((eig, eig), f32),
-            pltpu.VMEM((subs - 1, eig, eig), f32),
             pltpu.VMEM((eig, eig), f32),
-            pltpu.VMEM((blks - 1, eig, eig), f32),
+            pltpu.VMEM((subs - 1, eig // subs, eig), f32),
+            pltpu.VMEM((eig // subs, eig), f32),
+            pltpu.VMEM((blks - 1, eig // subs, eig), f32),
+            pltpu.VMEM((eig // subs, eig), f32),
+            pltpu.VMEM((subs, eig // subs, eig), f32),
             dma((subs - 1,)), dma((subs - 1,)),
+            dma((half,)), dma((half,)),
             dma((half,)), dma((half,)),
             dma((half, 2)), dma((half, 2)),
             dma((half,)), dma((half,)),
             dma((links,)), dma((links,)),
             dma((links,)), dma((links,)),
             dma((links,)), dma((links,)),
-            dma((subs + blks - 2,)), dma((subs + blks - 2,)),
+            dma((2 * subs + blks - 3,)), dma((2 * subs + blks - 3,)),
         ],
         compiler_params=pltpu.CompilerParams(
             collective_id=0, has_side_effects=True, vmem_limit_bytes=56 * 1024 * 1024

time: 115 us -> 106 us (0.922)
  Pallas kernels: 111 us -> 102 us
    pallas_call x1, Pallas kernels: 111 us -> 102 us  [local(): pl.pallas_call(functools.partial(kernel, blks, subs, half, feat_dim), out...]
where the time goes in v3:
time: 106 us; the launch traced here: 105 us
  Pallas kernels  102 us (96%)
  matrix products  1.77 us (2%)
  local copies, waits for them, and re-layouts  1.31 us (1%)
    pallas_call x1, Pallas kernels, local(): pl.pallas_call(functools.partial(kernel, blks, subs, half, feat_dim), out...  102 us

profile of v3, /device:TPU:0, one launch (start us, length us, event | category | flops | bytes accessed | tf_op | source)
XLA Modules:
  0.0 105.4 jit_solution(11457378016102686659)
XLA Ops:
  0.0 1.3 %broadcast_in_dim.2.scale_rows = f32[8,1536]{1,0:T(8,128)} broadcast(bf16[1536]{0:T(1024)(128)(2,1)} %param.5), dimensions={1} | broadcast | bytes 52224 | tf_op jit(solution)/shard_map/broadcast_in_dim | solution.py:357
  1.3 102.3 %shard_map.46 = (f32[64,384]{1,0:T(8,128)}, f32[64,64]{1,0:T(8,128)}) custom-call(bf16[384,768]{1,0:T(8,128)(2,1)} %feats.1, s32[9,16,1536]{2,1,0:T(8,128)} %lists.1, f32[8,1536]{1,0:T(8,128)} %broadcast_in_dim.2.scale_rows, f32[64,384]{1,0:T(8,128)} %eigen.1), custom_call_target="tpu_custom_call" | custom-call | tf_op jit(solution)/shard_map/pallas_call | solution.py:361
  103.6 1.8 %fusion = f32[64,384]{1,0:T(8,128)} fusion(f32[64,64]{1,0:T(8,128)} %get-tuple-element.7, f32[64,384]{1,0:T(8,128)} %get-tuple-element.8), kind=kOutput, calls=%fused_computation | convolution fusion | flops 18874368 | bytes 212992 | tf_op jit(solution)/shard_map/dot_general | solution.py:408
